TPU v7x, 32 devices: a whole 2x2x4 slice. The times are simulated.
32 devices in a mesh: ctx: 8 (over y, x, core), fsdp: 4 (over z).
Axes of the slice: x: 2, y: 2, z: 4, core: 2. Of those that a mesh axis runs over, the one named last changes fastest.
Arguments:
- tokens: bfloat16 [4, 4096, 768], P('fsdp', 'ctx'), may hold values from -6 to 6
- cotangent: bfloat16 [4, 4096, 768], P('fsdp', 'ctx'), may hold values from -6 to 6
- lengths: int32 [4, 4], P('fsdp'), may hold values from 1 to 2048, 4096 in all within a row
- dealing: int32 [4, 16], P('fsdp'), may hold values from 0 to 15, each once within a row
- qkv_weight: bfloat16 [768, 2304], P('fsdp'), may hold values from -0.21875 to 0.21875
- out_weight: bfloat16 [768, 768], P('fsdp'), may hold values from -0.21875 to 0.21875
- in_weight: bfloat16 [768, 3072], P('fsdp'), may hold values from -0.21875 to 0.21875
- back_weight: bfloat16 [3072, 768], P('fsdp'), may hold values from -0.109375 to 0.109375
- norm_gains: bfloat16 [3, 768], P(None, 'fsdp'), may hold values from 0.25 to 1.75
- shifts: bfloat16 [7, 768], P(None, 'fsdp'), may hold values from -1.796875 to 1.796875
- ffn_gain: bfloat16 [3072], P('fsdp'), may hold values from 0.25 to 1.75
- ffn_shifts: bfloat16 [2, 3072], P(None, 'fsdp'), may hold values from -1.796875 to 1.796875
Outputs:
- mixed_out: bfloat16 [4, 4096, 768], P('fsdp', 'ctx')
- input_grad: float32 [4, 4096, 768], P('fsdp', 'ctx')
- qkv_grad: float32 [768, 2304], P(('ctx', 'fsdp'))
- out_grad: float32 [768, 768], P(('ctx', 'fsdp'))
- in_grad: float32 [768, 3072], P(('ctx', 'fsdp'))
- back_grad: float32 [3072, 768], P(('ctx', 'fsdp'))
- gains_grad: float32 [3, 768], P(None, ('ctx', 'fsdp'))
- shifts_grad: float32 [7, 768], P(None, ('ctx', 'fsdp'))
- ffn_gain_grad: float32 [3072], P(('ctx', 'fsdp'))
- ffn_shifts_grad: float32 [2, 3072], P(None, ('ctx', 'fsdp'))
Inputs may be any that keep to these rules, and one draw needn't show every extreme that they name: `lengths`: each row sums to 4096 and its largest entry is exactly 2048. `dealing`: each row is a permutation of the group numbers.
All inputs are finite; a program needn't handle non-finite values.
Results may differ from a plain program's by a relative error of at most 0.018.
Values may be sent and summed in bfloat16 or wider, within the bound.
No kernel may reach another device: no remote copies, remote signals or barrier semaphores. Data moves between devices by JAX's collectives and lax.ppermute only.
A program may use at most 256 MiB of HBM per device.

v0:
```python
import math
import jax
import jax.numpy as jnp
from jax import lax
from jax.sharding import PartitionSpec as P

D = 768
H = 12
DH = 64


def layer_norm(values, gain, shift):
    average = jnp.mean(values, axis=-1, keepdims=True)
    centred = values - average
    variance = jnp.mean(centred * centred, axis=-1, keepdims=True)
    return centred * lax.rsqrt(variance + 1e-05) * gain + shift


def gelu_exact(values):
    return jax.nn.gelu(values, approximate=False)


def row_places(first_row, row_count, deal_row, bounds, group_rows):
    row_ids = first_row + jnp.arange(row_count, dtype=jnp.int32)
    group_ids = row_ids // group_rows
    onehot = (group_ids[:, None] == jnp.arange(deal_row.shape[0], dtype=jnp.int32)[None, :]).astype(
        jnp.int32
    )
    picked = jnp.sum(onehot * deal_row[None, :], axis=1)
    places = picked * group_rows + row_ids % group_rows
    segment = jnp.sum((places[:, None] >= bounds[None, :]).astype(jnp.int32), axis=1)
    return (places, segment)


def outer_sum(left, right):
    return lax.dot_general(
        left, right, (((0,), (0,)), ((), ())), preferred_element_type=jnp.float32
    )


def times_transposed(left, matrix):
    return lax.dot_general(
        left, matrix, (((1,), (1,)), ((), ())), preferred_element_type=jnp.float32
    )


def unpack(loaded):
    qkv_w, out_w, in_w, back_w, gains, shift_rows, ffn_gain, ffn_shift_rows = loaded
    return (
        qkv_w,
        out_w,
        in_w,
        back_w,
        gains.astype(jnp.float32),
        shift_rows.astype(jnp.float32),
        ffn_gain.astype(jnp.float32),
        ffn_shift_rows.astype(jnp.float32),
    )


def local(
    tokens,
    cotangent,
    lengths,
    dealing,
    qkv_weight,
    out_weight,
    in_weight,
    back_weight,
    norm_gains,
    shifts,
    ffn_gain,
    ffn_shifts,
):
    position = lax.axis_index("ctx")
    tok_rows = tokens.shape[1]
    group_rows = tok_rows // 2
    deal_row = dealing[0]
    bounds = jnp.cumsum(lengths[0])
    scaling = DH ** (-0.5)
    loaded = (
        lax.all_gather(qkv_weight, "fsdp", axis=0, tiled=True),
        lax.all_gather(out_weight, "fsdp", axis=0, tiled=True),
        lax.all_gather(in_weight, "fsdp", axis=0, tiled=True),
        lax.all_gather(back_weight, "fsdp", axis=0, tiled=True),
        lax.all_gather(norm_gains, "fsdp", axis=1, tiled=True),
        lax.all_gather(shifts, "fsdp", axis=1, tiled=True),
        lax.all_gather(ffn_gain, "fsdp", axis=0, tiled=True),
        lax.all_gather(ffn_shifts, "fsdp", axis=1, tiled=True),
    )
    qkv_w, out_w, in_w, back_w, gains, shift_rows, ffn_scale, ffn_shift_rows = unpack(loaded)
    inputs = tokens[0].astype(jnp.float32)
    normed = layer_norm(inputs, gains[0], shift_rows[0])
    normed_low = normed.astype(jnp.bfloat16)
    projected = jnp.dot(normed_low, qkv_w, preferred_element_type=jnp.float32)
    query = (projected[:, :D] + shift_rows[1]).astype(jnp.bfloat16)
    keyed = projected[:, D : 2 * D].astype(jnp.bfloat16)
    valued = (projected[:, 2 * D :] + shift_rows[2]).astype(jnp.bfloat16)
    query3 = query.reshape(tok_rows, H, DH)
    q_places, q_segment = row_places(position * tok_rows, tok_rows, deal_row, bounds, group_rows)

    def allowed_pairs(qp, qs, k_places, k_segment):
        return ((k_segment[None, :] == qs[:, None]) & (k_places[None, :] <= qp[:, None]))[None]

    initial = (
        jnp.full((H, tok_rows), -1e30, jnp.float32),
        jnp.zeros((H, tok_rows), jnp.float32),
        jnp.zeros((H, tok_rows, DH), jnp.float32),
    )
    key_rows = lax.all_gather(keyed, "ctx", axis=0, tiled=True)
    value_rows = lax.all_gather(valued, "ctx", axis=0, tiled=True)
    key_count = key_rows.shape[0]
    block_rows = 512
    block_count = key_count // block_rows
    k_places, k_segment = row_places(jnp.int32(0), key_count, deal_row, bounds, group_rows)
    stacked = (
        key_rows.reshape(block_count, block_rows, H, DH),
        value_rows.reshape(block_count, block_rows, H, DH),
        k_places.reshape(block_count, block_rows),
        k_segment.reshape(block_count, block_rows),
    )

    def visit_block(inner_state, pieces):
        maxima, totals, weighted = inner_state
        key3, value3, block_places, block_segment = pieces
        scores = (
            jnp.einsum("qhd,khd->hqk", query3, key3, preferred_element_type=jnp.float32) * scaling
        )
        allowed = allowed_pairs(q_places, q_segment, block_places, block_segment)
        masked = jnp.where(allowed, scores, -1e30)
        raised = jnp.maximum(maxima, jnp.max(masked, axis=-1))
        rescale = jnp.exp(maxima - raised)
        expo = jnp.where(allowed, jnp.exp(masked - raised[..., None]), 0.0)
        totals = totals * rescale + jnp.sum(expo, axis=-1)
        weighted = weighted * rescale[..., None] + jnp.einsum(
            "hqk,khd->hqd", expo.astype(jnp.bfloat16), value3, preferred_element_type=jnp.float32
        )
        return ((raised, totals, weighted), None)

    maxima, totals, weighted = lax.scan(visit_block, initial, stacked)[0]
    context3 = weighted / totals[..., None]
    log_total = maxima + jnp.log(totals)
    context = context3.transpose(1, 0, 2).reshape(tok_rows, D)
    inner = layer_norm(context, gains[1], shift_rows[3])
    inner_low = inner.astype(jnp.bfloat16)
    branch = jnp.dot(inner_low, out_w, preferred_element_type=jnp.float32) + shift_rows[4]
    middle = inputs + branch
    normed_two = layer_norm(middle, gains[2], shift_rows[5])
    normed_two_low = normed_two.astype(jnp.bfloat16)
    hidden = jnp.dot(normed_two_low, in_w, preferred_element_type=jnp.float32) + ffn_shift_rows[0]
    activated = gelu_exact(hidden)
    inner_two = layer_norm(activated, ffn_scale, ffn_shift_rows[1])
    inner_two_low = inner_two.astype(jnp.bfloat16)
    result = jnp.dot(inner_two_low, back_w, preferred_element_type=jnp.float32) + shift_rows[6]
    mixed_out = (middle + result).astype(jnp.bfloat16)
    loaded_back = (
        lax.all_gather(qkv_weight, "fsdp", axis=0, tiled=True),
        lax.all_gather(out_weight, "fsdp", axis=0, tiled=True),
        lax.all_gather(in_weight, "fsdp", axis=0, tiled=True),
        lax.all_gather(back_weight, "fsdp", axis=0, tiled=True),
        lax.all_gather(norm_gains, "fsdp", axis=1, tiled=True),
        lax.all_gather(shifts, "fsdp", axis=1, tiled=True),
        lax.all_gather(ffn_gain, "fsdp", axis=0, tiled=True),
        lax.all_gather(ffn_shifts, "fsdp", axis=1, tiled=True),
    )
    qkv_w, out_w, in_w, back_w, gains, shift_rows, ffn_scale, ffn_shift_rows = unpack(loaded_back)
    upstream = cotangent[0].astype(jnp.float32)
    result_low = cotangent[0]
    grad_back_w = outer_sum(inner_two_low, result_low)
    grad_back_bias = jnp.sum(result_low.astype(jnp.float32), axis=0)
    grad_inner_two = times_transposed(result_low, back_w)
    norm_pull = jax.vjp(layer_norm, activated, ffn_scale, ffn_shift_rows[1])[1]
    grad_activated, grad_ffn_gain, grad_ffn_shift = norm_pull(grad_inner_two)
    gelu_pull = jax.vjp(gelu_exact, hidden)[1]
    grad_hidden = gelu_pull(grad_activated)[0]
    hidden_low = grad_hidden.astype(jnp.bfloat16)
    grad_in_w = outer_sum(normed_two_low, hidden_low)
    grad_in_bias = jnp.sum(hidden_low.astype(jnp.float32), axis=0)
    grad_normed_two = times_transposed(hidden_low, in_w)
    second_pull = jax.vjp(layer_norm, middle, gains[2], shift_rows[5])[1]
    grad_middle_part, grad_gain_two, grad_shift_five = second_pull(grad_normed_two)
    grad_middle = upstream + grad_middle_part
    branch_low = grad_middle.astype(jnp.bfloat16)
    grad_out_w = outer_sum(inner_low, branch_low)
    grad_out_bias = jnp.sum(branch_low.astype(jnp.float32), axis=0)
    grad_inner = times_transposed(branch_low, out_w)
    inner_pull = jax.vjp(layer_norm, context, gains[1], shift_rows[3])[1]
    grad_context, grad_gain_one, grad_shift_three = inner_pull(grad_inner)
    context_grad_low = grad_context.astype(jnp.bfloat16).reshape(tok_rows, H, DH)
    delta = jnp.einsum("qhd,hqd->hq", context_grad_low.astype(jnp.float32), context3)

    def grad_pair(
        q_rows, grad_rows, lse_rows, delta_rows, qp, qs, key3, value3, k_places, k_segment
    ):
        scores = (
            jnp.einsum("qhd,khd->hqk", q_rows, key3, preferred_element_type=jnp.float32) * scaling
        )
        allowed = allowed_pairs(qp, qs, k_places, k_segment)
        probabilities = jnp.where(allowed, jnp.exp(scores - lse_rows[..., None]), 0.0)
        upstream_probs = jnp.einsum(
            "qhd,khd->hqk", grad_rows, value3, preferred_element_type=jnp.float32
        )
        score_grad = (probabilities * (upstream_probs - delta_rows[..., None])).astype(jnp.bfloat16)
        query_add = (
            jnp.einsum("hqk,khd->qhd", score_grad, key3, preferred_element_type=jnp.float32)
            * scaling
        )
        key_add = (
            jnp.einsum("hqk,qhd->khd", score_grad, q_rows, preferred_element_type=jnp.float32)
            * scaling
        )
        value_add = jnp.einsum(
            "hqk,qhd->khd",
            probabilities.astype(jnp.bfloat16),
            grad_rows,
            preferred_element_type=jnp.float32,
        )
        return (query_add, key_add, value_add)

    def grad_block(key3, value3, k_places, k_segment):
        return grad_pair(
            query3,
            context_grad_low,
            log_total,
            delta,
            q_places,
            q_segment,
            key3,
            value3,
            k_places,
            k_segment,
        )

    zero_query = jnp.zeros((tok_rows, H, DH), jnp.float32)
    gathered_keys, gathered_values = (
        lax.all_gather(keyed, "ctx", axis=0, tiled=True),
        lax.all_gather(valued, "ctx", axis=0, tiled=True),
    )
    stream_rows = gathered_keys.shape[0]
    block_rows = math.gcd(stream_rows, 512)
    block_count = stream_rows // block_rows
    all_places, all_segment = row_places(0, stream_rows, deal_row, bounds, group_rows)

    def sweep(query_grad, pieces):
        key3, value3, block_places, block_segment = pieces
        query_add, key_add, value_add = grad_block(key3, value3, block_places, block_segment)
        return (query_grad + query_add, (key_add, value_add))

    query_grad, (key_parts, value_parts) = lax.scan(
        sweep,
        zero_query,
        (
            gathered_keys.reshape(block_count, block_rows, H, DH),
            gathered_values.reshape(block_count, block_rows, H, DH),
            all_places.reshape(block_count, block_rows),
            all_segment.reshape(block_count, block_rows),
        ),
    )
    key_terms = key_parts.reshape(stream_rows, D)
    value_terms = value_parts.reshape(stream_rows, D)
    key_grad_mine, value_grad_mine = (
        lax.psum_scatter(
            key_terms.astype(jnp.bfloat16), "ctx", scatter_dimension=0, tiled=True
        ).astype(jnp.float32),
        lax.psum_scatter(
            value_terms.astype(jnp.bfloat16), "ctx", scatter_dimension=0, tiled=True
        ).astype(jnp.float32),
    )
    qkv_grad_low = jnp.concatenate(
        [query_grad.reshape(tok_rows, D), key_grad_mine, value_grad_mine], axis=1
    ).astype(jnp.bfloat16)
    grad_qkv_w = outer_sum(normed_low, qkv_grad_low)
    column_sums = jnp.sum(qkv_grad_low.astype(jnp.float32), axis=0)
    grad_query_bias = column_sums[:D]
    grad_value_bias = column_sums[2 * D :]
    grad_normed = times_transposed(qkv_grad_low, qkv_w)
    first_pull = jax.vjp(layer_norm, inputs, gains[0], shift_rows[0])[1]
    grad_inputs_part, grad_gain_zero, grad_shift_zero = first_pull(grad_normed)
    input_grad = grad_middle + grad_inputs_part
    gains_terms = jnp.stack([grad_gain_zero, grad_gain_one, grad_gain_two])
    shift_terms = jnp.stack(
        [
            grad_shift_zero,
            grad_query_bias,
            grad_value_bias,
            grad_shift_three,
            grad_out_bias,
            grad_shift_five,
            grad_back_bias,
        ]
    )
    ffn_shift_terms = jnp.stack([grad_in_bias, grad_ffn_shift])
    reduced = (
        lax.psum_scatter(grad_qkv_w, ("ctx", "fsdp"), scatter_dimension=0, tiled=True),
        lax.psum_scatter(grad_out_w, ("ctx", "fsdp"), scatter_dimension=0, tiled=True),
        lax.psum_scatter(grad_in_w, ("ctx", "fsdp"), scatter_dimension=0, tiled=True),
        lax.psum_scatter(grad_back_w, ("ctx", "fsdp"), scatter_dimension=0, tiled=True),
        lax.psum_scatter(gains_terms, ("ctx", "fsdp"), scatter_dimension=1, tiled=True),
        lax.psum_scatter(shift_terms, ("ctx", "fsdp"), scatter_dimension=1, tiled=True),
        lax.psum_scatter(grad_ffn_gain, ("ctx", "fsdp"), scatter_dimension=0, tiled=True),
        lax.psum_scatter(ffn_shift_terms, ("ctx", "fsdp"), scatter_dimension=1, tiled=True),
    )
    return (mixed_out[None], input_grad[None]) + tuple(reduced)


def solution(mesh):
    in_specs = (
        P("fsdp", "ctx", None),
        P("fsdp", "ctx", None),
        P("fsdp", None),
        P("fsdp", None),
        P("fsdp", None),
        P("fsdp", None),
        P("fsdp", None),
        P("fsdp", None),
        P(None, "fsdp"),
        P(None, "fsdp"),
        P("fsdp"),
        P(None, "fsdp"),
    )
    out_specs = (
        P("fsdp", "ctx", None),
        P("fsdp", "ctx", None),
        P(("ctx", "fsdp"), None),
        P(("ctx", "fsdp"), None),
        P(("ctx", "fsdp"), None),
        P(("ctx", "fsdp"), None),
        P(None, ("ctx", "fsdp")),
        P(None, ("ctx", "fsdp")),
        P(("ctx", "fsdp")),
        P(None, ("ctx", "fsdp")),
    )
    return jax.shard_map(local, mesh=mesh, in_specs=in_specs, out_specs=out_specs, check_vma=False)
```

profile of v0, /device:TPU:0, one launch (start us, length us, event | category | flops | bytes accessed | tf_op | source)
XLA Modules:
  0.0 1461.5 jit_solution(8794208688010352200)
XLA Ops:
  8.0 14.9 %all-gather.1 = bf16[4,192,7]{1,2,0:T(8,128)(2,1)S(1)} all-gather(bf16[1,192,7]{1,2,0:T(8,128)(2,1)} %bitcast.267), channel_id=1, replica_groups=mesh['ctx'=8,'fsdp'=4] {'fsdp'}, dimensions={0}, use_global_device_ids=true | all-gather | bytes 13440 | tf_op jit(solution)/shard_map/all_gather | solution.py:87
  23.0 12.2 all-gather
  38.9 43.6 %all-gather.10.cloned.1.call-done = bf16[768,2304]{1,0:T(8,128)(2,1)} async-done(((bf16[192,2304]{1,0:T(8,128)(2,1)}), bf16[768,2304]{1,0:T(8,128)(2,1)}) %all-gather.10.cloned.1.call-update) | async-done | bytes 3538960 | tf_op jit(solution)/shard_map/all_gather | solution.py:82
  95.8 13.0 all_gather.45
  109.5 13.6 all-gather.2
  124.2 10.1 all-gather.12.cloned.1.call-done
  134.3 8.6 copy.91
  155.3 26.5 %all-gather.14.cloned.1.call-done = bf16[4096,768]{1,0:T(8,128)(2,1)} async-done(((bf16[512,768]{1,0:T(8,128)(2,1)}), bf16[4096,768]{1,0:T(8,128)(2,1)}) %all-gather.14.cloned.1.call-update) | async-done | bytes 6291472 | tf_op jit(solution)/shard_map/all_gather | solution.py:111
  181.8 8.9 copy.93
  202.6 179.3 %while.30 = (s32[]{:T(128)}, f32[12,512]{1,0:T(8,128)S(1)}, f32[12,512]{1,0:T(8,128)S(1)}, f32[12,512,64]{1,2,0:T(8,128)}, s32[8,512]{1,0:T(8,128)S(1)}, /*index...) while((s32[]{:T(128)}, f32[12,512]{1,0:T(8,128)S(1)}, ...), condition=%wide.region_10.11_spmd.clone, body=%wide.region_7.10_spmd.clone.sunk | while | flops 848197632 | bytes 95043760 | solution.py:140
  389.9 21.5 %fusion.101 = (f32[512]{0:T(512)S(1)}, f32[512,3072]{1,0:T(8,128)}, f32[512,3072]{1,0:T(8,128)}, f32[512,3072]{1,0:T(8,128)}) fusion(f32[3072]{0:T(1024)S(1)} %bitcast.261, bf16[768,3072]{1,0:T(8,128)(2,1)} %all-gather.18.cloned.1.call-done, f32[512,768]{1,0:T(8,128)} %copy-done.10, f32[768]{0:T(1024)S(1)} %get-tuple-element.371, ...), kind=kOutput, calls=%fused_computation.205 | convolution fusion | flops 2521693696 | bytes 25190400 | tf_op jit(solution)/shard_map/dot_general | solution.py:150
  422.2 10.8 convert_reduce_fusion
  447.7 251.0 %while.31 = (s32[]{:T(128)}, f32[512,12,64]{0,2,1:T(8,128)}, bf16[8,512,12,64]{1,3,2,0:T(8,128)(2,1)}, bf16[8,512,12,64]{1,3,2,0:T(8,128)(2,1)}, bf16[8,512,12,6...) while((s32[]{:T(128)}, f32[512,12,64]{0,2,1:T(8,128)}, ...), condition=%wide.region_24.25_spmd.clone, body=%wide.region_23.24_spmd.clone.sunk | while | flops 2047082496 | bytes 195125520 | solution.py:249
  486.7 8.4 fusion.165
  580.8 8.4 fusion.165
  612.1 8.4 fusion.165
  750.1 24.5 %reduce-scatter.14.cloned.1.call-done = bf16[512,768]{0,1:T(8,128)(2,1)} async-done(((bf16[4096,768]{0,1:T(8,128)(2,1)}), bf16[512,768]{0,1:T(8,128)(2,1)}) %reduce-scatter.14.cloned.1.call-update) | async-done | bytes 786448 | tf_op jit(solution)/shard_map/reduce_scatter | solution.py:265
  774.6 65.5 %reduce-scatter.12.cloned.1.call-done = bf16[512,768]{0,1:T(8,128)(2,1)} async-done(((bf16[4096,768]{0,1:T(8,128)(2,1)}), bf16[512,768]{0,1:T(8,128)(2,1)}) %reduce-scatter.12.cloned.1.call-update) | async-done | bytes 786448 | tf_op jit(solution)/shard_map/reduce_scatter | solution.py:262
  855.0 87.4 %reduce-scatter.24.cloned.1.call-done = f32[96,2]{1,0:T(8,128)} async-done(((f32[3072,2]{1,0:T(8,128)}), f32[96,2]{1,0:T(8,128)}) %reduce-scatter.24.cloned.1.call-update) | async-done | bytes 784
  952.3 40.7 %all-reduce.3 = (f32[3,768]{1,0:T(4,128)S(1)}, f32[7,768]{1,0:T(8,128)S(1)}, f32[3072]{0:T(1024)S(1)}) all-reduce(f32[3,768]{1,0:T(4,128)S(1)} %pad_maximum_fusion.2, f32[7,768]{1,0:T(8,128)S(1)} %stack.36, f32[3072]{0:T(1024)S(1)} %copy-done.25), channel_id=8, replica_groups=mesh['ctx'=8,'fsdp'=4] {'ctx','fsdp'}, use_global_device_ids=true, to_apply=%region_36.37.clone | all-reduce | flops 10752 | bytes 86016
  994.9 51.3 %reduce-scatter.18.cloned.1.call-done = f32[24,768]{1,0:T(8,128)} async-done(((f32[768,768]{1,0:T(8,128)}), f32[24,768]{1,0:T(8,128)}) %reduce-scatter.18.cloned.1.call-update) | async-done | bytes 73744 | tf_op jit(solution)/shard_map/reduce_scatter | solution.py:295
  1046.2 142.2 %reduce-scatter.20.cloned.1.call-done = f32[24,3072]{1,0:T(8,128)} async-done(((f32[768,3072]{1,0:T(8,128)}), f32[24,3072]{1,0:T(8,128)}) %reduce-scatter.20.cloned.1.call-update) | async-done | bytes 294928 | tf_op jit(solution)/shard_map/reduce_scatter | solution.py:296
  1188.4 140.8 %reduce-scatter.22.cloned.1.call-done = f32[96,768]{1,0:T(8,128)} async-done(((f32[3072,768]{1,0:T(8,128)}), f32[96,768]{1,0:T(8,128)}) %reduce-scatter.22.cloned.1.call-update) | async-done | bytes 294928 | tf_op jit(solution)/shard_map/reduce_scatter | solution.py:297
  1329.2 125.6 %reduce-scatter.16.cloned.1.call-done = f32[24,2304]{1,0:T(8,128)} async-done(((f32[768,2304]{1,0:T(8,128)}), f32[24,2304]{1,0:T(8,128)}) %reduce-scatter.16.cloned.1.call-update) | async-done | bytes 221200 | tf_op jit(solution)/shard_map/reduce_scatter | solution.py:294
  (411 shorter events, 558.4 us)
Async XLA Ops:
  7.2 75.3 %all-gather.10.cloned.1.call-start = ((), (), s32[]{:S(2)}) async-start(), calls=%async_computation.7 | async-start | bytes 4423680 | tf_op jit(solution)/shard_map/all_gather | solution.py:82
  7.9 126.4 %all-gather.12.cloned.1.call-start = ((), (), s32[]{:S(2)}) async-start(), calls=%async_computation.8 | async-start | bytes 7077888 | tf_op jit(solution)/shard_map/all_gather | solution.py:110
  35.4 51.5 %copy-start.26 = (f32[768]{0:T(1024)}, f32[768]{0:T(1024)S(1)}, u32[]{:S(2)}) copy-start(f32[768]{0:T(1024)S(1)} %get-tuple-element.379) | copy-start | bytes 9220
  36.0 50.9 %copy-start.39 = (f32[768]{0:T(1024)}, f32[768]{0:T(1024)S(1)}, u32[]{:S(2)}) copy-start(f32[768]{0:T(1024)S(1)} %get-tuple-element.376) | copy-start | bytes 9220
  36.0 349.6 %copy-start.43 = (f32[768]{0:T(1024)}, f32[768]{0:T(1024)S(1)}, u32[]{:S(2)}) copy-start(f32[768]{0:T(1024)S(1)} %get-tuple-element.373) | copy-start | bytes 9220
  36.0 353.9 %copy-start.41 = (f32[768]{0:T(1024)}, f32[768]{0:T(1024)S(1)}, u32[]{:S(2)}) copy-start(f32[768]{0:T(1024)S(1)} %get-tuple-element.371) | copy-start | bytes 9220
  37.3 49.5 %copy-start.28 = (f32[512]{0:T(512)}, f32[512]{0:T(512)S(1)}, u32[]{:S(2)}) copy-start(f32[512]{0:T(512)S(1)} %broadcast_multiply_fusion.4) | copy-start | bytes 6148
  38.8 48.0 %copy-start.32 = (f32[512]{0:T(512)}, f32[512]{0:T(512)S(1)}, u32[]{:S(2)}) copy-start(f32[512]{0:T(512)S(1)} %fusion.57) | copy-start | bytes 6148
  90.1 91.7 %all-gather.14.cloned.1.call-start = ((), (), s32[]{:S(2)}) async-start(), calls=%async_computation.9 | async-start | bytes 7077888 | tf_op jit(solution)/shard_map/all_gather | solution.py:111
  93.2 292.3 %all-gather.16.cloned.1.call-start = ((), (), s32[]{:S(2)}) async-start(), calls=%async_computation.10 | async-start | bytes 1474560 | tf_op jit(solution)/shard_map/all_gather | solution.py:83
  93.8 296.1 %all-gather.18.cloned.1.call-start = ((), (), s32[]{:S(2)}) async-start(), calls=%async_computation.11 | async-start | bytes 5898240 | tf_op jit(solution)/shard_map/all_gather | solution.py:84
  94.4 317.0 %all-gather.20.cloned.1.call-start = ((), (), s32[]{:S(2)}) async-start(), calls=%async_computation.12 | async-start | bytes 5898240 | tf_op jit(solution)/shard_map/all_gather | solution.py:85
  94.9 679.7 %reduce-scatter.14.cloned.1.call-start = ((), (), s32[]{:S(2)}) async-start(), calls=%async_computation.14 | async-start | bytes 7077888 | tf_op jit(solution)/shard_map/reduce_scatter | solution.py:265
  712.4 127.7 %reduce-scatter.12.cloned.1.call-start = ((), (), s32[]{:S(2)}) async-start(), calls=%async_computation.13 | async-start | bytes 7077888 | tf_op jit(solution)/shard_map/reduce_scatter | solution.py:262
  727.0 215.4 %reduce-scatter.24.cloned.1.call-start = ((), (), s32[]{:S(2)}) async-start(), calls=%async_computation.19 | async-start | bytes 1622016
  729.4 316.8 %reduce-scatter.18.cloned.1.call-start = ((), (), s32[]{:S(2)}) async-start(), calls=%async_computation.16 | async-start | bytes 2433024 | tf_op jit(solution)/shard_map/reduce_scatter | solution.py:295
  733.2 455.3 %reduce-scatter.20.cloned.1.call-start = ((), (), s32[]{:S(2)}) async-start(), calls=%async_computation.17 | async-start | bytes 9732096 | tf_op jit(solution)/shard_map/reduce_scatter | solution.py:296
  740.5 588.7 %reduce-scatter.22.cloned.1.call-start = ((), (), s32[]{:S(2)}) async-start(), calls=%async_computation.18 | async-start | bytes 9732096 | tf_op jit(solution)/shard_map/reduce_scatter | solution.py:297
  748.6 91.6 %copy-start.9 = (bf16[1,512,768]{2,1,0:T(8,128)(2,1)S(1)}, bf16[1,512,768]{2,1,0:T(8,128)(2,1)}, u32[]{:S(2)}) copy-start(bf16[1,512,768]{2,1,0:T(8,128)(2,1)} %param.16) | copy-start | bytes 2359300
  748.6 91.6 %copy-start.27 = (f32[768]{0:T(1024)S(1)}, f32[768]{0:T(1024)}, u32[]{:S(2)}) copy-start(f32[768]{0:T(1024)} %copy-done.26) | copy-start | bytes 9220
  748.6 91.6 %copy-start.29 = (f32[512]{0:T(512)S(1)}, f32[512]{0:T(512)}, u32[]{:S(2)}) copy-start(f32[512]{0:T(512)} %copy-done.28) | copy-start | bytes 6148
  748.6 91.6 %copy-start.31 = (f32[512]{0:T(512)S(1)}, f32[512]{0:T(512)}, u32[]{:S(2)}) copy-start(f32[512]{0:T(512)} %copy-done.30) | copy-start | bytes 6148
  748.6 91.6 %copy-start.40 = (f32[768]{0:T(1024)S(1)}, f32[768]{0:T(1024)}, u32[]{:S(2)}) copy-start(f32[768]{0:T(1024)} %copy-done.39) | copy-start | bytes 9220
  748.6 706.2 %reduce-scatter.16.cloned.1.call-start = ((), (), s32[]{:S(2)}) async-start(), calls=%async_computation.15 | async-start | bytes 7299072 | tf_op jit(solution)/shard_map/reduce_scatter | solution.py:294
  (71 other events, 431.7 us)
Sparse Core Ops, SparseCore 0:
  9.6 72.8 all-gather.9
  90.2 44.0 all-gather.11
  136.2 45.5 all-gather.13
  183.2 30.4 all-gather.15
  215.1 88.5 all-gather.17
  305.1 87.8 all-gather.19
  712.5 62.0 reduce-scatter.13
  778.4 61.7 reduce-scatter.11
  845.4 96.9 reduce-scatter.23
  948.1 98.0 reduce-scatter.17
  1053.7 134.6 reduce-scatter.19
  1194.8 134.4 reduce-scatter.21
  1336.4 118.3 reduce-scatter.15
where the time goes:
time: 1470 us; the launch traced here: 1460 us
  waiting for transfers between devices  720 us (49%)
  matrix products  403 us (27%)
  local copies, waits for them, and re-layouts  131 us (9%)
  other arithmetic  96.1 us (7%)
  blocking collectives  94.5 us (6%)
  between operations  14.9 us (1%)
    reduce_scatter x1, waiting for transfers between devices, local(): lax.psum_scatter(grad_in_w, ('ctx', 'fsdp'), scatter_dimension=0, tiled=T...  142 us
    reduce_scatter x1, waiting for transfers between devices, local(): lax.psum_scatter(grad_back_w, ('ctx', 'fsdp'), scatter_dimension=0, tiled...  141 us
    reduce_scatter x1, waiting for transfers between devices, local(): lax.psum_scatter(grad_qkv_w, ('ctx', 'fsdp'), scatter_dimension=0, tiled=...  126 us
    unnamed x14, waiting for transfers between devices  89.8 us
    dot_general x8, matrix products, grad_pair(): jnp.einsum('qhd,khd->hqk', grad_rows, value3, preferred_element_type=jnp....  67.5 us
    reduce_scatter x1, waiting for transfers between devices, local(): lax.psum_scatter(key_terms.astype(jnp.bfloat16), 'ctx', scatter_dimension...  65.5 us
    dot_general x8, matrix products, visit_block(): jnp.einsum('qhd,khd->hqk', query3, key3, preferred_element_type=jnp.float32)  64 us
    reduce_sum x8, other arithmetic, visit_block(): totals = totals * rescale + jnp.sum(expo, axis=-1)  61.3 us
  transfers between devices with their start and end apart: 13, of which 10 were waited for; matrix products, arithmetic and copies ran while one was open for 21% of the time, Pallas kernels for 0%

commit v1 on v0

--- a/solution.py
+++ b/solution.py
@@ -7,6 +7,19 @@
 D = 768
 H = 12
 DH = 64
+
+
+def gather_around(shard, axis, dim):
+    ways = lax.axis_size(axis)
+    up = [(d, (d + 1) % ways) for d in range(ways)]
+    down = [(d, (d - 1) % ways) for d in range(ways)]
+    earlier, later = ([shard], [shard])
+    for _ in range(ways // 2):
+        earlier.append(lax.ppermute(earlier[-1], axis, up))
+    for _ in range((ways - 1) // 2):
+        later.append(lax.ppermute(later[-1], axis, down))
+    line = jnp.concatenate([*earlier[::-1], *later[1:]], axis=dim)
+    return jnp.roll(line, (lax.axis_index(axis) - ways // 2) * shard.shape[dim], axis=dim)
 
 
 def layer_norm(values, gain, shift):
@@ -108,7 +121,7 @@
         jnp.zeros((H, tok_rows, DH), jnp.float32),
     )
     key_rows = lax.all_gather(keyed, "ctx", axis=0, tiled=True)
-    value_rows = lax.all_gather(valued, "ctx", axis=0, tiled=True)
+    value_rows = gather_around(valued, "ctx", 0)
     key_count = key_rows.shape[0]
     block_rows = 512
     block_count = key_count // block_rows

time: 1470 us -> 1550 us (1.054)
  waiting for transfers between devices: 720 us -> 755 us
  local copies, waits for them, and re-layouts: 131 us -> 163 us
    ppermute x0 -> x7, waiting for transfers between devices: none -> 69.7 us  [the longest x4 51.2 us: gather_around(): earlier.append(lax.ppermute(earlier[-1], axis, up))]
    all_gather x1, waiting for transfers between devices: 26.5 us -> 0.02 us  [local(): lax.all_gather(valued, 'ctx', axis=0, tiled=True)]
    unnamed x112 -> x141, local copies, waits for them, and re-layouts: 54 us -> 73.7 us
  transfers between devices with their start and end apart: 13 -> 20, of which waited for: 10 -> 12; matrix products, arithmetic and copies ran while one was open for 21% -> 22% of each run, Pallas kernels for 0% -> 0%
where the time goes in v1:
time: 1550 us; the launch traced here: 1540 us
  waiting for transfers between devices  755 us (49%)
  matrix products  406 us (26%)
  local copies, waits for them, and re-layouts  163 us (11%)
  other arithmetic  96.3 us (6%)
  blocking collectives  94.3 us (6%)
    reduce_scatter x1, waiting for transfers between devices, local(): lax.psum_scatter(grad_in_w, ('ctx', 'fsdp'), scatter_dimension=0, tiled=T...  142 us
    reduce_scatter x1, waiting for transfers between devices, local(): lax.psum_scatter(grad_back_w, ('ctx', 'fsdp'), scatter_dimension=0, tiled...  141 us
    reduce_scatter x1, waiting for transfers between devices, local(): lax.psum_scatter(grad_qkv_w, ('ctx', 'fsdp'), scatter_dimension=0, tiled=...  125 us
    unnamed x14, waiting for transfers between devices  90 us
    unnamed x141, local copies, waits for them, and re-layouts  73.7 us
    dot_general x8, matrix products, grad_pair(): jnp.einsum('qhd,khd->hqk', grad_rows, value3, preferred_element_type=jnp....  67.5 us
    reduce_scatter x1, waiting for transfers between devices, local(): lax.psum_scatter(key_terms.astype(jnp.bfloat16), 'ctx', scatter_dimension...  65.5 us
    dot_general x8, matrix products, visit_block(): jnp.einsum('qhd,khd->hqk', query3, key3, preferred_element_type=jnp.float32)  65.4 us
  transfers between devices with their start and end apart: 20, of which 12 were waited for; matrix products, arithmetic and copies ran while one was open for 22% of the time, Pallas kernels for 0%

profile of v1, /device:TPU:0, one launch (start us, length us, event | category | flops | bytes accessed | tf_op | source)
XLA Modules:
  0.0 1538.7 jit_solution(12226995607455905103)
XLA Ops:
  8.0 14.9 all-gather.1
  23.0 12.2 all-gather
  38.9 43.6 %all-gather.10.cloned.1.call-done = bf16[768,2304]{1,0:T(8,128)(2,1)} async-done(((bf16[192,2304]{1,0:T(8,128)(2,1)}), bf16[768,2304]{1,0:T(8,128)(2,1)}) %all-gather.10.cloned.1.call-update) | async-done | bytes 3538960 | tf_op jit(solution)/shard_map/all_gather | solution.py:95
  94.3 20.7 %collective-permute-done = bf16[512,768]{1,0:T(8,128)(2,1)S(1)} collective-permute-done((bf16[512,768]{1,0:T(8,128)(2,1)S(1)}, bf16[512,768]{1,0:T(8,128)(2,1)S(1)}, u32[]{:S(2)}, u32[]{:S(2)}) %collective-permute-start) | collective-permute-done | bytes 786464 | tf_op jit(solution)/shard_map/ppermute | solution.py:18
  118.0 30.4 %collective-permute-done.1 = bf16[512,768]{1,0:T(8,128)(2,1)S(1)} collective-permute-done((bf16[512,768]{1,0:T(8,128)(2,1)S(1)}, bf16[512,768]{1,0:T(8,128)(2,1)S(1)}, u32[]{:S(2)}, u32[]{:S(2)}) %collective-permute-start.1) | collective-permute-done | bytes 786464 | tf_op jit(solution)/shard_map/ppermute | solution.py:18
  148.6 13.0 all-gather.2
  162.3 13.3 all_gather.43
  178.2 13.8 collective-permute-done.5
  212.9 8.6 copy.95
  233.5 8.8 copy.93
  254.1 181.0 %while.30 = (s32[]{:T(128)}, f32[12,512]{1,0:T(8,128)S(1)}, f32[12,512]{1,0:T(8,128)S(1)}, f32[12,512,64]{1,2,0:T(8,128)}, s32[8,512]{1,0:T(8,128)S(1)}, /*index...) while((s32[]{:T(128)}, f32[12,512]{1,0:T(8,128)S(1)}, ...), condition=%wide.region_10.11_spmd.clone, body=%wide.region_7.10_spmd.clone.sunk | while | flops 848197632 | bytes 95043760 | solution.py:153
  276.5 8.6 fusion.150
  443.1 21.6 %fusion.101 = (f32[512]{0:T(512)S(1)}, f32[512,3072]{1,0:T(8,128)}, f32[512,3072]{1,0:T(8,128)}, f32[512,3072]{1,0:T(8,128)}) fusion(f32[3072]{0:T(1024)S(1)} %bitcast.270, bf16[768,3072]{1,0:T(8,128)(2,1)} %all-gather.16.cloned.1.call-done, f32[512,768]{1,0:T(8,128)} %copy-done.13, f32[768]{0:T(1024)S(1)} %get-tuple-element.371, ...), kind=kOutput, calls=%fused_computation.222 | convolution fusion | flops 2521693696 | bytes 25190400 | tf_op jit(solution)/shard_map/dot_general | solution.py:163
  475.3 8.9 copy.99
  496.4 11.4 convert_reduce_fusion
  522.1 251.5 %while.31 = (s32[]{:T(128)}, f32[512,12,64]{0,2,1:T(8,128)}, bf16[8,512,12,64]{1,3,2,0:T(8,128)(2,1)}, bf16[8,512,12,64]{1,3,2,0:T(8,128)(2,1)}, bf16[8,512,12,6...) while((s32[]{:T(128)}, f32[512,12,64]{0,2,1:T(8,128)}, ...), condition=%wide.region_24.25_spmd.clone, body=%wide.region_23.24_spmd.clone.sunk | while | flops 2047082496 | bytes 195125520 | solution.py:262
  825.2 26.7 %reduce-scatter.14.cloned.1.call-done = bf16[512,768]{0,1:T(8,128)(2,1)} async-done(((bf16[4096,768]{0,1:T(8,128)(2,1)}), bf16[512,768]{0,1:T(8,128)(2,1)}) %reduce-scatter.14.cloned.1.call-update) | async-done | bytes 786448 | tf_op jit(solution)/shard_map/reduce_scatter | solution.py:278
  851.9 65.5 %reduce-scatter.12.cloned.1.call-done = bf16[512,768]{0,1:T(8,128)(2,1)} async-done(((bf16[4096,768]{0,1:T(8,128)(2,1)}), bf16[512,768]{0,1:T(8,128)(2,1)}) %reduce-scatter.12.cloned.1.call-update) | async-done | bytes 786448 | tf_op jit(solution)/shard_map/reduce_scatter | solution.py:275
  932.3 87.4 %reduce-scatter.24.cloned.1.call-done = f32[96,2]{1,0:T(8,128)} async-done(((f32[3072,2]{1,0:T(8,128)}), f32[96,2]{1,0:T(8,128)}) %reduce-scatter.24.cloned.1.call-update) | async-done | bytes 784
  1029.4 40.8 %all-reduce.3 = (f32[3,768]{1,0:T(4,128)S(1)}, f32[7,768]{1,0:T(8,128)S(1)}, f32[3072]{0:T(1024)S(1)}) all-reduce(f32[3,768]{1,0:T(4,128)S(1)} %pad_maximum_fusion.2, f32[7,768]{1,0:T(8,128)S(1)} %stack.36, f32[3072]{0:T(1024)S(1)} %copy-done.29), channel_id=8, replica_groups=mesh['ctx'=8,'fsdp'=4] {'ctx','fsdp'}, use_global_device_ids=true, to_apply=%region_36.37.clone | all-reduce | flops 10752 | bytes 86016
  1072.1 51.4 %reduce-scatter.18.cloned.1.call-done = f32[24,768]{1,0:T(8,128)} async-done(((f32[768,768]{1,0:T(8,128)}), f32[24,768]{1,0:T(8,128)}) %reduce-scatter.18.cloned.1.call-update) | async-done | bytes 73744 | tf_op jit(solution)/shard_map/reduce_scatter | solution.py:308
  1123.5 142.1 %reduce-scatter.20.cloned.1.call-done = f32[24,3072]{1,0:T(8,128)} async-done(((f32[768,3072]{1,0:T(8,128)}), f32[24,3072]{1,0:T(8,128)}) %reduce-scatter.20.cloned.1.call-update) | async-done | bytes 294928 | tf_op jit(solution)/shard_map/reduce_scatter | solution.py:309
  1265.6 141.0 %reduce-scatter.22.cloned.1.call-done = f32[96,768]{1,0:T(8,128)} async-done(((f32[3072,768]{1,0:T(8,128)}), f32[96,768]{1,0:T(8,128)}) %reduce-scatter.22.cloned.1.call-update) | async-done | bytes 294928 | tf_op jit(solution)/shard_map/reduce_scatter | solution.py:310
  1406.6 125.3 %reduce-scatter.16.cloned.1.call-done = f32[24,2304]{1,0:T(8,128)} async-done(((f32[768,2304]{1,0:T(8,128)}), f32[24,2304]{1,0:T(8,128)}) %reduce-scatter.16.cloned.1.call-update) | async-done | bytes 221200 | tf_op jit(solution)/shard_map/reduce_scatter | solution.py:307
  (458 shorter events, 611.7 us)
Async XLA Ops:
  7.2 75.3 %all-gather.10.cloned.1.call-start = ((), (), s32[]{:S(2)}) async-start(), calls=%async_computation.7 | async-start | bytes 4423680 | tf_op jit(solution)/shard_map/all_gather | solution.py:95
  7.9 225.6 %all-gather.12.cloned.1.call-start = ((), (), s32[]{:S(2)}) async-start(), calls=%async_computation.8 | async-start | bytes 7077888 | tf_op jit(solution)/shard_map/all_gather | solution.py:123
  36.0 402.8 %copy-start.47 = (f32[768]{0:T(1024)}, f32[768]{0:T(1024)S(1)}, u32[]{:S(2)}) copy-start(f32[768]{0:T(1024)S(1)} %get-tuple-element.373) | copy-start | bytes 9220
  36.0 407.1 %copy-start.45 = (f32[768]{0:T(1024)}, f32[768]{0:T(1024)S(1)}, u32[]{:S(2)}) copy-start(f32[768]{0:T(1024)S(1)} %get-tuple-element.371) | copy-start | bytes 9220
  90.1 348.7 %all-gather.14.cloned.1.call-start = ((), (), s32[]{:S(2)}) async-start(), calls=%async_computation.9 | async-start | bytes 1474560 | tf_op jit(solution)/shard_map/all_gather | solution.py:96
  90.8 352.2 %all-gather.16.cloned.1.call-start = ((), (), s32[]{:S(2)}) async-start(), calls=%async_computation.10 | async-start | bytes 5898240 | tf_op jit(solution)/shard_map/all_gather | solution.py:97
  91.4 373.3 %all-gather.18.cloned.1.call-start = ((), (), s32[]{:S(2)}) async-start(), calls=%async_computation.11 | async-start | bytes 5898240 | tf_op jit(solution)/shard_map/all_gather | solution.py:98
  92.0 383.3 %all-gather.20.cloned.1.call-start = ((), (), s32[]{:S(2)}) async-start(), calls=%async_computation.12 | async-start | bytes 7077888 | tf_op jit(solution)/shard_map/all_gather | solution.py:250
  94.2 20.8 %collective-permute-start = (bf16[512,768]{1,0:T(8,128)(2,1)S(1)}, bf16[512,768]{1,0:T(8,128)(2,1)S(1)}, u32[]{:S(2)}, u32[]{:S(2)}) collective-permute-start(bf16[512,768]{1,0:T(8,128)(2,1)S(1)} %get-tuple-element.455), channel_id=1, source_target_pairs={{0,4},{4,8},{8,12},{12,16},{16,20},{20,24},{24,28},{28,0},{1,5},{5... | collective-permute-start | bytes 2359304 | tf_op jit(solution)/shard_map/ppermute | solution.py:18
  115.0 33.5 %collective-permute-start.1 = (bf16[512,768]{1,0:T(8,128)(2,1)S(1)}, bf16[512,768]{1,0:T(8,128)(2,1)S(1)}, u32[]{:S(2)}, u32[]{:S(2)}) collective-permute-start(bf16[512,768]{1,0:T(8,128)(2,1)S(1)} %collective-permute-done), channel_id=1, source_target_pairs={{0,4},{4,8},{8,12},{12,16},{16,20},{20,24},{24,28},{28,0},{1,5},{5... | collective-permute-start | bytes 2359304 | tf_op jit(solution)/shard_map/ppermute | solution.py:18
  115.3 60.4 %collective-permute-start.4 = (bf16[512,768]{1,0:T(8,128)(2,1)S(1)}, bf16[512,768]{1,0:T(8,128)(2,1)}, u32[]{:S(2)}, u32[]{:S(2)}) collective-permute-start(bf16[512,768]{1,0:T(8,128)(2,1)S(1)} %get-tuple-element.455), channel_id=1, source_target_pairs={{0,28},{4,0},{8,4},{12,8},{16,12},{20,16},{24,20},{28,24},{1,29},{... | collective-permute-start | bytes 2359304 | tf_op jit(solution)/shard_map/ppermute | solution.py:20
  148.4 27.3 %collective-permute-start.2 = (bf16[512,768]{1,0:T(8,128)(2,1)S(1)}, bf16[512,768]{1,0:T(8,128)(2,1)}, u32[]{:S(2)}, u32[]{:S(2)}) collective-permute-start(bf16[512,768]{1,0:T(8,128)(2,1)S(1)} %collective-permute-done.1), channel_id=1, source_target_pairs={{0,4},{4,8},{8,12},{12,16},{16,20},{20,24},{24,28},{28,0},{1,5},{5... | collective-permute-start | bytes 2359304 | tf_op jit(solution)/shard_map/ppermute | solution.py:18
  175.7 16.3 %collective-permute-start.5 = (bf16[512,768]{1,0:T(8,128)(2,1)}, bf16[512,768]{1,0:T(8,128)(2,1)}, u32[]{:S(2)}, u32[]{:S(2)}) collective-permute-start(bf16[512,768]{1,0:T(8,128)(2,1)} %collective-permute-done.4), channel_id=1, source_target_pairs={{0,28},{4,0},{8,4},{12,8},{16,12},{20,16},{24,20},{28,24},{1,29},{... | collective-permute-start | bytes 2359304 | tf_op jit(solution)/shard_map/ppermute | solution.py:20
  175.8 19.2 %collective-permute-start.3 = (bf16[512,768]{1,0:T(8,128)(2,1)}, bf16[512,768]{1,0:T(8,128)(2,1)}, u32[]{:S(2)}, u32[]{:S(2)}) collective-permute-start(bf16[512,768]{1,0:T(8,128)(2,1)} %collective-permute-done.2), channel_id=1, source_target_pairs={{0,4},{4,8},{8,12},{12,16},{16,20},{20,24},{24,28},{28,0},{1,5},{5... | collective-permute-start | bytes 2359304 | tf_op jit(solution)/shard_map/ppermute | solution.py:18
  178.2 673.7 %reduce-scatter.14.cloned.1.call-start = ((), (), s32[]{:S(2)}) async-start(), calls=%async_computation.14 | async-start | bytes 7077888 | tf_op jit(solution)/shard_map/reduce_scatter | solution.py:278
  192.0 12.8 collective-permute-start.6
  787.5 129.9 %reduce-scatter.12.cloned.1.call-start = ((), (), s32[]{:S(2)}) async-start(), calls=%async_computation.13 | async-start | bytes 7077888 | tf_op jit(solution)/shard_map/reduce_scatter | solution.py:275
  801.9 217.8 %reduce-scatter.24.cloned.1.call-start = ((), (), s32[]{:S(2)}) async-start(), calls=%async_computation.19 | async-start | bytes 1622016
  804.3 319.2 %reduce-scatter.18.cloned.1.call-start = ((), (), s32[]{:S(2)}) async-start(), calls=%async_computation.16 | async-start | bytes 2433024 | tf_op jit(solution)/shard_map/reduce_scatter | solution.py:308
  808.0 457.6 %reduce-scatter.20.cloned.1.call-start = ((), (), s32[]{:S(2)}) async-start(), calls=%async_computation.17 | async-start | bytes 9732096 | tf_op jit(solution)/shard_map/reduce_scatter | solution.py:309
  815.6 591.0 %reduce-scatter.22.cloned.1.call-start = ((), (), s32[]{:S(2)}) async-start(), calls=%async_computation.18 | async-start | bytes 9732096 | tf_op jit(solution)/shard_map/reduce_scatter | solution.py:310
  823.7 93.7 %copy-start.31 = (f32[768]{0:T(1024)S(1)}, f32[768]{0:T(1024)}, u32[]{:S(2)}) copy-start(f32[768]{0:T(1024)} %copy-done.30) | copy-start | bytes 9220
  823.7 93.7 %copy-start.33 = (f32[512]{0:T(512)S(1)}, f32[512]{0:T(512)}, u32[]{:S(2)}) copy-start(f32[512]{0:T(512)} %copy-done.32) | copy-start | bytes 6148
  823.8 708.1 %reduce-scatter.16.cloned.1.call-start = ((), (), s32[]{:S(2)}) async-start(), calls=%async_computation.15 | async-start | bytes 7299072 | tf_op jit(solution)/shard_map/reduce_scatter | solution.py:307
  (84 other events, 1234.1 us)
Sparse Core Ops, SparseCore 0:
  9.6 72.8 all-gather.9
  90.2 63.9 all-gather.11
  155.8 29.3 all-gather.13
  186.6 88.9 all-gather.15
  277.0 87.8 all-gather.17
  366.6 43.9 all-gather.19
  787.6 64.2 reduce-scatter.13
  855.6 61.7 reduce-scatter.11
  922.7 96.9 reduce-scatter.23
  1025.4 98.0 reduce-scatter.17
  1131.0 134.5 reduce-scatter.19
  1271.9 134.5 reduce-scatter.21
  1413.8 118.0 reduce-scatter.15
